TPU v7x, 32 devices: a whole 2x2x4 slice. The times are simulated.
32 devices in a mesh: group: 4 (over y, x), dp: 2 (over core), tensor: 4 (over z).
Axes of the slice: x: 2, y: 2, z: 4, core: 2. Of those that a mesh axis runs over, the one named last changes fastest.
Arguments:
- tokens: bfloat16 [8192, 2048], P(('group', 'dp')), may hold values from -6 to 6
- norm_gain: bfloat16 [2048], replicated, may hold values from 0.099609375 to 1.8984375
- w_query: bfloat16 [2048, 2048], P(None, 'tensor'), may hold values from -0.25 to 0.25
- w_keyval: bfloat16 [2048, 512], P(None, 'tensor'), may hold values from -0.125 to 0.125
- w_out: bfloat16 [2048, 2048], P('tensor'), may hold values from -0.8984375 to 0.8984375
- kv_cache: bfloat16 [4, 32, 16, 128, 512], P(None, ('group', 'dp'), None, None, 'tensor'), may hold values from -400 to 400
- lengths: int32 [32, 2], P(('group', 'dp')), may hold values from 0 to 2048, as said below
- dest_slot: int32 [32, 16], replicated, may hold values from 0 to 511, as said below
Outputs:
- mixed: bfloat16 [8192, 2048], P(('group', 'dp', 'tensor'))
- decode_cache: bfloat16 [4, 512, 128, 512], P(None, ('group', 'dp'), None, 'tensor')
Inputs may be any that keep to these rules, and one draw needn't show every extreme that they name: lengths[p, 0] lies in 0 to 2048 and lengths[p, 1] in 1 to 256; 2048 and 256 are each taken by some prompt; the prompts r * 4 to r * 4 + 3 of each index r of group and dp together hold exactly 32 live blocks. dest_slot is a permutation of the 512 slots; the slots of the index r of group and dp together are r * 4 * 16 onward; the blocks of prompts r * 4 to r * 4 + 3 send exactly 8 blocks to each index, of which exactly 4 is live.
All inputs are finite; a program needn't handle non-finite values.
Results may differ from a plain program's by a relative error of at most 0.009.
Values may be sent and summed in bfloat16 or wider, within the bound.
A program may use at most 128 MiB of HBM per device.

v0:
```python
import jax
import jax.numpy as jnp
from jax import lax
from jax.sharding import PartitionSpec as P

HD = 64


def per_device(tokens, norm_gain, w_query, w_keyval, w_out, kv_cache, lengths, dest_slot):
    tok_rows = tokens.shape[0]
    prompts = lengths.shape[0]
    fresh_rows = tok_rows // prompts
    heads_local = w_query.shape[1] // HD
    kv_local = w_keyval.shape[1] // (2 * HD)
    group_size = heads_local // kv_local
    layers = kv_cache.shape[0]
    blocks_win = kv_cache.shape[2]
    block_len = kv_cache.shape[3]
    lane_width = kv_cache.shape[4]
    window = blocks_win * block_len
    tokens_f = tokens.astype(jnp.float32)
    normed = (
        tokens_f
        * lax.rsqrt(jnp.mean(tokens_f * tokens_f, axis=-1, keepdims=True) + 1e-05)
        * norm_gain.astype(jnp.float32)
    ).astype(jnp.bfloat16)
    query = jnp.dot(normed, w_query, preferred_element_type=jnp.float32).astype(jnp.bfloat16)
    query = query.reshape(prompts, fresh_rows, kv_local, group_size, HD)
    keyval = jnp.dot(normed, w_keyval, preferred_element_type=jnp.float32).astype(jnp.bfloat16)
    keyval = keyval.reshape(prompts, fresh_rows, kv_local, 2, HD)
    cache = kv_cache[0].reshape(prompts, window, kv_local, 2, HD)
    scale = 1.0 / HD**0.5
    query_pos = jnp.arange(fresh_rows)[:, None]
    key_pos = jnp.arange(window + fresh_rows)[None, :]

    def attend(items):
        query_p, cache_p, fresh_p, history, fresh_len = items
        pairs = jnp.concatenate([cache_p, fresh_p], axis=0)
        scores = (
            jnp.einsum(
                "ckgd,tkd->kgct", query_p, pairs[:, :, 0], preferred_element_type=jnp.float32
            )
            * scale
        )
        visible = jnp.where(
            key_pos < window,
            (key_pos >= window - history) & (key_pos >= query_pos + 1),
            key_pos - window <= query_pos,
        )
        scores = jnp.where(visible, scores, -1e30)
        scores = scores - jnp.max(scores, axis=-1, keepdims=True)
        expo = jnp.exp(scores)
        weights = (expo / jnp.sum(expo, axis=-1, keepdims=True)).astype(jnp.bfloat16)
        mixed_p = jnp.einsum(
            "kgct,tkd->ckgd", weights, pairs[:, :, 1], preferred_element_type=jnp.float32
        )
        mixed_p = mixed_p.astype(jnp.bfloat16).reshape(fresh_rows, heads_local * HD)
        return jnp.where(
            (jnp.arange(fresh_rows) < fresh_len)[:, None], mixed_p, jnp.zeros_like(mixed_p)
        )

    attn = lax.map(attend, (query, cache, keyval, lengths[:, 0], lengths[:, 1]))
    attn = attn.reshape(tok_rows, heads_local * HD)
    mixed = lax.psum_scatter(
        jnp.dot(attn, w_out, preferred_element_type=jnp.float32),
        "tensor",
        scatter_dimension=0,
        tiled=True,
    ).astype(jnp.bfloat16)
    per_dev = prompts * blocks_win
    devices = lax.axis_size(("group", "dp"))
    per_peer = per_dev // devices
    my_index = lax.axis_index(("group", "dp"))
    dest_all = dest_slot.reshape(devices, per_dev)
    recv_all = dest_all // per_dev
    same_dest = recv_all[:, :, None] == recv_all[:, None, :]
    earlier = jnp.arange(per_dev)[None, :] < jnp.arange(per_dev)[:, None]
    own_recv = lax.dynamic_index_in_dim(recv_all, my_index, 0, keepdims=False)
    senders = jnp.arange(devices, dtype=jnp.int32)[:, None]
    capacity = per_peer // 2
    lengths_every = lax.all_gather(lengths, ("group", "dp"), axis=0, tiled=True)
    live_all = (
        (jnp.arange(blocks_win)[None, :] + 1) * block_len > window - lengths_every[:, 0:1]
    ).reshape(devices, per_dev)
    live_rank = jnp.sum(same_dest & earlier[None, :, :] & live_all[:, None, :], axis=2)
    own_live = lax.dynamic_index_in_dim(live_all, my_index, 0, keepdims=False)
    own_live_rank = lax.dynamic_index_in_dim(live_rank, my_index, 0, keepdims=False)
    send_pos = jnp.where(own_live, own_recv * capacity + own_live_rank, devices * capacity)
    send_idx = (
        jnp.zeros((devices * capacity,), jnp.int32)
        .at[send_pos]
        .set(jnp.arange(per_dev, dtype=jnp.int32), mode="drop")
    )
    raw_blocks = kv_cache.reshape(layers, per_dev, block_len, lane_width)
    outgoing = jnp.take(raw_blocks, send_idx, axis=1)
    incoming = lax.all_to_all(outgoing, ("group", "dp"), split_axis=1, concat_axis=1, tiled=True)
    where_from = senders * capacity + live_rank
    valid = (recv_all == my_index) & live_all
    slot_local = jnp.where(valid, dest_all - my_index * per_dev, per_dev)
    source_idx = (
        jnp.full((per_dev,), devices * capacity, jnp.int32)
        .at[slot_local.reshape(-1)]
        .set(where_from.reshape(-1), mode="drop")
    )
    decode_cache = jnp.take(incoming, source_idx, axis=1, mode="fill", fill_value=0)
    return (mixed, decode_cache)


def solution(mesh):
    in_specs = (
        P(("group", "dp"), None),
        P(),
        P(None, "tensor"),
        P(None, "tensor"),
        P("tensor", None),
        P(None, ("group", "dp"), None, None, "tensor"),
        P(("group", "dp"), None),
        P(),
    )
    out_specs = (P(("group", "dp", "tensor"), None), P(None, ("group", "dp"), None, "tensor"))
    return jax.shard_map(
        per_device, mesh=mesh, in_specs=in_specs, out_specs=out_specs, check_vma=False
    )
```

profile of v0, /device:TPU:0, one launch (start us, length us, event | category | flops | bytes accessed | tf_op | source)
XLA Modules:
  0.0 344.5 jit_solution(16174500329635103676)
XLA Ops:
  7.2 1.4 slice_bitcast_fusion
  8.6 3.2 slice.25
  11.8 4.5 %copy.51 = bf16[1,4,16,128,128]{3,2,4,1,0:T(8,128)(2,1)} copy(bf16[1,4,16,128,128]{4,3,2,1,0:T(8,128)(2,1)} %slice.25) | data formatting | bytes 4194304 | tf_op jit(solution)/shard_map/slice | solution.py:31
  16.3 4.2 %reshape_squeeze.3 = bf16[4,2048,1,2,64]{1,4,3,2,0:T(8,128)(2,1)} reshape(bf16[1,4,16,128,128]{3,2,4,1,0:T(8,128)(2,1)} %copy.51) | data formatting | bytes 4194304 | tf_op jit(solution)/shard_map/reshape;squeeze | solution.py:31
  20.4 3.1 fusion.27
  23.5 3.6 %fusion.33 = bf16[1024,128]{1,0:T(8,128)(2,1)S(1)} fusion(bf16[2048,128]{1,0:T(8,128)(2,1)} %param.13, bf16[1024,2048]{1,0:T(8,128)(2,1)} %param.10, f32[2048]{0:T(1024)S(1)} %convert_element_type.40, f32[1024]{0:T(1024)S(1)} %add_rsqrt_fusion), kind=kOutput, calls=%fused_computation.51 | convolution fusion | flops 545390592 | bytes 4993024 | tf_op jit(solution)/shard_map/dot_general | solution.py:29
  27.1 0.2 reshape.480
  27.4 0.3 copy.54
  27.7 5.3 %convolution_convert_fusion = bf16[1024,512]{1,0:T(8,128)(2,1)S(1)} fusion(bf16[2048,512]{1,0:T(8,128)(2,1)} %param.12, bf16[1024,2048]{1,0:T(8,128)(2,1)} %param.10, f32[2048]{0:T(1024)S(1)} %convert_element_type.40, f32[1024]{0:T(1024)S(1)} %add_rsqrt_fusion), kind=kOutput, calls=%fused_computation.49 | convolution fusion | flops 2156396544 | bytes 7352320 | tf_op jit(solution)/shard_map/dot_general | solution.py:27
  33.0 2.1 reshape.481
  35.1 3.0 copy.55
  38.1 142.6 %while.14 = (s32[]{:T(128)}, bf16[4,256,512]{2,1,0:T(8,128)(2,1)}, s32[4]{0:T(128)}, bf16[4,2048,1,2,64]{1,4,3,2,0:T(8,128)(2,1)}, bf16[4,256,1,2,64]{1,4,3,2,0:...) while((s32[]{:T(128)}, bf16[4,256,512]{2,1,0:T(8,128)(2,1)}, ...), condition=%wide.region_4.5_spmd.clone.clone, body=%wide.region_1.4_spmd.clone.clone.sunk | while | flops 1268387072 | bytes 63510268 | solution.py:62
  38.1 1.3 dynamic_slice.91
  40.1 2.0 fusion.58
  42.2 1.1 dynamic-slice_bitcast_fusion.5
  43.3 9.0 %fusion.59 = (f32[8,256]{1,0:T(8,128)S(1)}, f32[2304,256,8]{1,0,2:T(8,128)}) fusion(pred[256,2304]{0,1:T(8,128)(4,1)S(1)} %fusion.58, bf16[4,256,1,8,64]{1,4,3,2,0:T(8,128)(2,1)} %get-tuple-element.310, s32[]{:T(128)S(6)} %copy.74, bf16[256,1,2,64]{0,3,2,1:T(8,128)(2,1)S(1)} %dynamic-slice_bitcast_fusion.4, ...), kind=kOutput, calls=%fused_computation.10.clone.1 | convolution fusion | flops 618723328 | bytes 20324356 | tf_op jit(solution)/shard_map/while/body/eval_jaxpr/ckgd,tkd->kgct/dot_general | solution.py:40
  52.3 10.2 %fusion.60 = f32[8,256]{1,0:T(8,128)S(1)} fusion(f32[2304,256,8]{1,0,2:T(8,128)} %get-tuple-element.284, f32[8,256]{1,0:T(8,128)S(1)} %get-tuple-element.285, pred[256,2304]{0,1:T(8,128)(4,1)S(1)} %fusion.58), kind=kLoop, calls=%fused_computation.9.clone.1 | loop fusion | flops 18872320 | bytes 19480576 | tf_op jit(solution)/shard_map/while/body/eval_jaxpr/reduce_sum | solution.py:53
  62.5 9.0 %fusion.61 = bf16[64,8,256]{2,0,1:T(8,128)(2,1)S(1)} fusion(f32[8,256]{1,0:T(8,128)S(1)} %fusion.60, f32[8,256]{1,0:T(8,128)S(1)} %get-tuple-element.285, f32[2304,256,8]{1,0,2:T(8,128)} %get-tuple-element.284, pred[256,2304]{0,1:T(8,128)(4,1)S(1)} %fusion.58, bf16[2048,1,2,64]{0,3,2,1:T(8,128)(2,1)S(1)} %dynamic-slice_bitcast_fusion.5, ...), kind=kOutput, calls=%fused_computation.17.clone.1 | convolution fusion | flops 628293632 | bytes 20332544 | tf_op jit(solution)/shard_map/while/body/eval_jaxpr/kgct,tkd->ckgd/dot_general | solution.py:54
  71.5 0.7 dynamic_slice.92
  72.2 0.7 iota_compare_fusion.9
  72.9 0.1 copy.70
  73.1 0.7 constant_dynamic-update-slice_fusion.2
  73.8 1.3 dynamic_slice.91
  75.8 2.0 fusion.58
  77.9 1.1 dynamic-slice_bitcast_fusion.5
  78.9 9.0 %fusion.59 = (f32[8,256]{1,0:T(8,128)S(1)}, f32[2304,256,8]{1,0,2:T(8,128)}) fusion(pred[256,2304]{0,1:T(8,128)(4,1)S(1)} %fusion.58, bf16[4,256,1,8,64]{1,4,3,2,0:T(8,128)(2,1)} %get-tuple-element.310, s32[]{:T(128)S(6)} %copy.74, bf16[256,1,2,64]{0,3,2,1:T(8,128)(2,1)S(1)} %dynamic-slice_bitcast_fusion.4, ...), kind=kOutput, calls=%fused_computation.10.clone.1 | convolution fusion | flops 618723328 | bytes 20324356 | tf_op jit(solution)/shard_map/while/body/eval_jaxpr/ckgd,tkd->kgct/dot_general | solution.py:40
  87.9 10.2 %fusion.60 = f32[8,256]{1,0:T(8,128)S(1)} fusion(f32[2304,256,8]{1,0,2:T(8,128)} %get-tuple-element.284, f32[8,256]{1,0:T(8,128)S(1)} %get-tuple-element.285, pred[256,2304]{0,1:T(8,128)(4,1)S(1)} %fusion.58), kind=kLoop, calls=%fused_computation.9.clone.1 | loop fusion | flops 18872320 | bytes 19480576 | tf_op jit(solution)/shard_map/while/body/eval_jaxpr/reduce_sum | solution.py:53
  98.1 9.0 %fusion.61 = bf16[64,8,256]{2,0,1:T(8,128)(2,1)S(1)} fusion(f32[8,256]{1,0:T(8,128)S(1)} %fusion.60, f32[8,256]{1,0:T(8,128)S(1)} %get-tuple-element.285, f32[2304,256,8]{1,0,2:T(8,128)} %get-tuple-element.284, pred[256,2304]{0,1:T(8,128)(4,1)S(1)} %fusion.58, bf16[2048,1,2,64]{0,3,2,1:T(8,128)(2,1)S(1)} %dynamic-slice_bitcast_fusion.5, ...), kind=kOutput, calls=%fused_computation.17.clone.1 | convolution fusion | flops 628293632 | bytes 20332544 | tf_op jit(solution)/shard_map/while/body/eval_jaxpr/kgct,tkd->ckgd/dot_general | solution.py:54
  107.2 0.7 dynamic_slice.92
  107.8 0.7 iota_compare_fusion.9
  108.7 0.7 constant_dynamic-update-slice_fusion.2
  109.5 1.3 dynamic_slice.91
  111.4 2.0 fusion.58
  113.5 1.1 dynamic-slice_bitcast_fusion.5
  114.6 9.0 %fusion.59 = (f32[8,256]{1,0:T(8,128)S(1)}, f32[2304,256,8]{1,0,2:T(8,128)}) fusion(pred[256,2304]{0,1:T(8,128)(4,1)S(1)} %fusion.58, bf16[4,256,1,8,64]{1,4,3,2,0:T(8,128)(2,1)} %get-tuple-element.310, s32[]{:T(128)S(6)} %copy.74, bf16[256,1,2,64]{0,3,2,1:T(8,128)(2,1)S(1)} %dynamic-slice_bitcast_fusion.4, ...), kind=kOutput, calls=%fused_computation.10.clone.1 | convolution fusion | flops 618723328 | bytes 20324356 | tf_op jit(solution)/shard_map/while/body/eval_jaxpr/ckgd,tkd->kgct/dot_general | solution.py:40
  123.6 10.2 %fusion.60 = f32[8,256]{1,0:T(8,128)S(1)} fusion(f32[2304,256,8]{1,0,2:T(8,128)} %get-tuple-element.284, f32[8,256]{1,0:T(8,128)S(1)} %get-tuple-element.285, pred[256,2304]{0,1:T(8,128)(4,1)S(1)} %fusion.58), kind=kLoop, calls=%fused_computation.9.clone.1 | loop fusion | flops 18872320 | bytes 19480576 | tf_op jit(solution)/shard_map/while/body/eval_jaxpr/reduce_sum | solution.py:53
  133.8 9.0 %fusion.61 = bf16[64,8,256]{2,0,1:T(8,128)(2,1)S(1)} fusion(f32[8,256]{1,0:T(8,128)S(1)} %fusion.60, f32[8,256]{1,0:T(8,128)S(1)} %get-tuple-element.285, f32[2304,256,8]{1,0,2:T(8,128)} %get-tuple-element.284, pred[256,2304]{0,1:T(8,128)(4,1)S(1)} %fusion.58, bf16[2048,1,2,64]{0,3,2,1:T(8,128)(2,1)S(1)} %dynamic-slice_bitcast_fusion.5, ...), kind=kOutput, calls=%fused_computation.17.clone.1 | convolution fusion | flops 628293632 | bytes 20332544 | tf_op jit(solution)/shard_map/while/body/eval_jaxpr/kgct,tkd->ckgd/dot_general | solution.py:54
  142.8 0.7 dynamic_slice.92
  143.5 0.7 iota_compare_fusion.9
  144.4 0.7 constant_dynamic-update-slice_fusion.2
  145.1 1.3 dynamic_slice.91
  147.1 2.0 fusion.58
  149.2 1.1 dynamic-slice_bitcast_fusion.5
  150.2 9.0 %fusion.59 = (f32[8,256]{1,0:T(8,128)S(1)}, f32[2304,256,8]{1,0,2:T(8,128)}) fusion(pred[256,2304]{0,1:T(8,128)(4,1)S(1)} %fusion.58, bf16[4,256,1,8,64]{1,4,3,2,0:T(8,128)(2,1)} %get-tuple-element.310, s32[]{:T(128)S(6)} %copy.74, bf16[256,1,2,64]{0,3,2,1:T(8,128)(2,1)S(1)} %dynamic-slice_bitcast_fusion.4, ...), kind=kOutput, calls=%fused_computation.10.clone.1 | convolution fusion | flops 618723328 | bytes 20324356 | tf_op jit(solution)/shard_map/while/body/eval_jaxpr/ckgd,tkd->kgct/dot_general | solution.py:40
  159.2 10.2 %fusion.60 = f32[8,256]{1,0:T(8,128)S(1)} fusion(f32[2304,256,8]{1,0,2:T(8,128)} %get-tuple-element.284, f32[8,256]{1,0:T(8,128)S(1)} %get-tuple-element.285, pred[256,2304]{0,1:T(8,128)(4,1)S(1)} %fusion.58), kind=kLoop, calls=%fused_computation.9.clone.1 | loop fusion | flops 18872320 | bytes 19480576 | tf_op jit(solution)/shard_map/while/body/eval_jaxpr/reduce_sum | solution.py:53
  169.4 9.0 %fusion.61 = bf16[64,8,256]{2,0,1:T(8,128)(2,1)S(1)} fusion(f32[8,256]{1,0:T(8,128)S(1)} %fusion.60, f32[8,256]{1,0:T(8,128)S(1)} %get-tuple-element.285, f32[2304,256,8]{1,0,2:T(8,128)} %get-tuple-element.284, pred[256,2304]{0,1:T(8,128)(4,1)S(1)} %fusion.58, bf16[2048,1,2,64]{0,3,2,1:T(8,128)(2,1)S(1)} %dynamic-slice_bitcast_fusion.5, ...), kind=kOutput, calls=%fused_computation.17.clone.1 | convolution fusion | flops 628293632 | bytes 20332544 | tf_op jit(solution)/shard_map/while/body/eval_jaxpr/kgct,tkd->ckgd/dot_general | solution.py:54
  178.5 0.7 dynamic_slice.92
  179.1 0.7 iota_compare_fusion.9
  180.0 0.7 constant_dynamic-update-slice_fusion.2
  180.8 6.8 %fusion.45 = f32[1024,2048]{1,0:T(8,128)} fusion(bf16[1024,512]{1,0:T(8,128)(2,1)} %bitcast.102, bf16[512,2048]{1,0:T(8,128)(2,1)S(1)} %copy-done), kind=kOutput, calls=%fused_computation.92 | convolution fusion | flops 2147483648 | bytes 11534336 | tf_op jit(solution)/shard_map/dot_general | solution.py:65
  187.8 10.3 %all-gather = s32[8,4,2]{1,2,0:T(2,128)S(1)} all-gather(s32[1,4,2]{1,2,0:T(2,128)S(1)} %bitcast.100), channel_id=1, replica_groups=mesh['group'=4,'dp'=2,'tensor'=4] {'group','dp'}, dimensions={0}, use_global_device_ids=true | all-gather | bytes 288 | tf_op jit(solution)/shard_map/all_gather | solution.py:81
  198.6 0.3 convert_reduce_fusion
  199.0 1.0 scatter_custom_fusion.1
  200.0 6.5 %gather_fusion = bf16[32,4,128,128]{3,2,1,0:T(8,128)(2,1)} fusion(bf16[4,64,128,128]{3,2,1,0:T(8,128)(2,1)} %bitcast.99, s32[1024]{0:T(1024)S(1)} %pad_clamp_fusion.1), kind=kCustom, calls=%fused_computation | custom fusion | bytes 8388736 | tf_op jit(solution)/shard_map/jit(_take)/gather | solution.py:95
  206.5 4.7 %select_bitcast_fusion.1 = bf16[4,32,128,128]{3,2,0,1:T(8,128)(2,1)} fusion(bf16[32,4,128,128]{3,2,1,0:T(8,128)(2,1)} %gather_fusion, pred[32]{0:T(512)(128)(4,1)S(1)} %compare_and_fusion), kind=kLoop, calls=%fused_computation.48 | loop fusion | flops 2097152 | bytes 8388640 | tf_op jit(solution)/shard_map/jit(_take)/select_n | solution.py:95
  211.1 4.6 %all-to-all-start = ((bf16[4,32,128,128]{3,2,0,1:T(8,128)(2,1)}), bf16[4,32,128,128]{3,2,0,1:T(8,128)(2,1)}, u32[]{:S(2)}, u32[]{:S(2)}) async-start(bf16[4,32,128,128]{3,2,0,1:T(8,128)(2,1)} %select_bitcast_fusion.1), calls=%async_computation.1 | async-start | bytes 8388608 | tf_op jit(solution)/shard_map/all_to_all | solution.py:96
  216.2 2.4 scatter_custom_fusion
  218.7 46.2 %all-to-all-done = bf16[4,32,128,128]{3,2,0,1:T(8,128)(2,1)} async-done(((bf16[4,32,128,128]{3,2,0,1:T(8,128)(2,1)}), bf16[4,32,128,128]{3,2,0,1:T(8,128)(2,1)}, u32[]{:S(2)}, u32[]{:S(2)}) %all-to-all-start) | async-done | bytes 4194336 | tf_op jit(solution)/shard_map/all_to_all | solution.py:96
  264.9 4.7 %copy.60 = bf16[4,32,128,128]{3,2,1,0:T(8,128)(2,1)} copy(bf16[4,32,128,128]{3,2,0,1:T(8,128)(2,1)} %all-to-all-done) | data formatting | bytes 8388608 | tf_op jit(solution)/shard_map/all_to_all | solution.py:96
  269.6 7.8 %gather_fusion.1 = bf16[64,4,128,128]{3,2,1,0:T(8,128)(2,1)} fusion(bf16[4,32,128,128]{3,2,1,0:T(8,128)(2,1)} %copy.60, s32[1024]{0:T(1024)S(1)} %pad_clamp_fusion), kind=kCustom, calls=%fused_computation.1 | custom fusion | bytes 16777472 | tf_op jit(solution)/shard_map/jit(_take)/gather | solution.py:105
  277.4 7.3 %select_bitcast_fusion = bf16[4,64,128,128]{3,2,0,1:T(8,128)(2,1)} fusion(bf16[64,4,128,128]{3,2,1,0:T(8,128)(2,1)} %gather_fusion.1, pred[64]{0:T(512)(128)(4,1)S(1)} %compare_and_fusion.1), kind=kLoop, calls=%fused_computation.47 | loop fusion | flops 4194304 | bytes 16777280 | tf_op jit(solution)/shard_map/jit(_take)/select_n | solution.py:105
  284.7 10.5 %copy.61 = bf16[4,64,128,128]{3,2,1,0:T(8,128)(2,1)} copy(bf16[4,64,128,128]{3,2,0,1:T(8,128)(2,1)} %select_bitcast_fusion) | data formatting | bytes 16777216
  295.2 39.7 %reduce-scatter.2.cloned.1.call-done = f32[256,2048]{1,0:T(8,128)} async-done(((f32[1024,2048]{1,0:T(8,128)}), f32[256,2048]{1,0:T(8,128)}) %reduce-scatter.2.cloned.1.call-update) | async-done | bytes 2097168 | tf_op jit(solution)/shard_map/reduce_scatter | solution.py:64
  334.9 2.7 convert_element_type.44
  (74 shorter events, 1.9 us)
Async XLA Ops:
  7.2 173.6 %copy-start = (bf16[512,2048]{1,0:T(8,128)(2,1)S(1)}, bf16[512,2048]{1,0:T(8,128)(2,1)}, u32[]{:S(2)}) copy-start(bf16[512,2048]{1,0:T(8,128)(2,1)} %param.14) | copy-start | bytes 6291460
  7.2 13.2 %copy-start.2 = (bf16[2048]{0:T(1024)(128)(2,1)S(1)}, bf16[2048]{0:T(1024)(128)(2,1)}, u32[]{:S(2)}) copy-start(bf16[2048]{0:T(1024)(128)(2,1)} %param.11) | copy-start | bytes 12292
  7.2 327.7 %reduce-scatter.2.cloned.1.call-start = ((), (), s32[]{:S(2)}) async-start(), calls=%async_computation.2 | async-start | bytes 10485760 | tf_op jit(solution)/shard_map/reduce_scatter | solution.py:64
  62.4 9.1 %copy-start.4 = (s32[4]{0:T(128)S(1)}, s32[4]{0:T(128)}, u32[]{:S(2)}) copy-start(s32[4]{0:T(128)} %get-tuple-element.306) | copy-start | bytes 52 | tf_op jit(solution)/shard_map/while
  98.1 9.1 %copy-start.4 = (s32[4]{0:T(128)S(1)}, s32[4]{0:T(128)}, u32[]{:S(2)}) copy-start(s32[4]{0:T(128)} %get-tuple-element.306) | copy-start | bytes 52 | tf_op jit(solution)/shard_map/while
  133.8 9.1 %copy-start.4 = (s32[4]{0:T(128)S(1)}, s32[4]{0:T(128)}, u32[]{:S(2)}) copy-start(s32[4]{0:T(128)} %get-tuple-element.306) | copy-start | bytes 52 | tf_op jit(solution)/shard_map/while
  169.4 9.1 %copy-start.4 = (s32[4]{0:T(128)S(1)}, s32[4]{0:T(128)}, u32[]{:S(2)}) copy-start(s32[4]{0:T(128)} %get-tuple-element.306) | copy-start | bytes 52 | tf_op jit(solution)/shard_map/while
  180.8 6.8 %copy-start.1 = (s32[32,16]{0,1:T(8,128)S(1)}, s32[32,16]{0,1:T(8,128)}, u32[]{:S(2)}) copy-start(s32[32,16]{0,1:T(8,128)} %param.17) | copy-start | bytes 6148
  180.8 7.0 %copy-start.3 = (s32[4,2]{0,1:T(2,128)S(1)}, s32[4,2]{0,1:T(2,128)}, u32[]{:S(2)}) copy-start(s32[4,2]{0,1:T(2,128)} %param.16) | copy-start | bytes 100
  211.1 53.7 %all-to-all-start = ((bf16[4,32,128,128]{3,2,0,1:T(8,128)(2,1)}), bf16[4,32,128,128]{3,2,0,1:T(8,128)(2,1)}, u32[]{:S(2)}, u32[]{:S(2)}) async-start(bf16[4,32,128,128]{3,2,0,1:T(8,128)(2,1)} %select_bitcast_fusion.1), calls=%async_computation.1 | async-start | bytes 8388608 | tf_op jit(solution)/shard_map/all_to_all | solution.py:96
Sparse Core Ops, SparseCore 0:
  187.7 147.1 reduce-scatter.1
where the time goes:
time: 346 us; the launch traced here: 344 us
  matrix products  87.7 us (25%)
  waiting for transfers between devices  85.9 us (25%)
  other arithmetic  70.1 us (20%)
  local copies, waits for them, and re-layouts  68.4 us (20%)
  between operations  14.2 us (4%)
  blocking collectives  10.3 us (3%)
  starting transfers between devices  4.64 us (1%)
    all_to_all x1, waiting for transfers between devices, per_device(): lax.all_to_all(outgoing, ('group', 'dp'), split_axis=1, concat_axis=1, ti...  46.2 us
    reduce_sum x4, other arithmetic, attend(): jnp.sum(expo, axis=-1, keepdims=True)  40.7 us
    reduce_scatter x1, waiting for transfers between devices, per_device(): lax.psum_scatter(jnp.dot(attn, w_out, preferred_element_type=jnp.float32)...  39.7 us
    dot_general x4, matrix products, attend(): jnp.einsum('kgct,tkd->ckgd', weights, pairs[:, :, 1], preferred_element_t...  36.2 us
    dot_general x4, matrix products, attend(): jnp.einsum('ckgd,tkd->kgct', query_p, pairs[:, :, 0], preferred_element_t...  35.9 us
    unnamed x13, local copies, waits for them, and re-layouts  14.1 us
    all_gather x1, blocking collectives, per_device(): lengths_every = lax.all_gather(lengths, ('group', 'dp'), axis=0, tiled=True)  10.3 us
    select_n x4, other arithmetic, attend(): jnp.where(key_pos < window, (key_pos >= window - history) & (key_pos >= q...  8.15 us
  transfers between devices with their start and end apart: 2, of which 2 were waited for; matrix products, arithmetic and copies ran while one was open for 13% of the time, Pallas kernels for 0%

commit v1 on v0

--- a/solution.py
+++ b/solution.py
@@ -4,6 +4,38 @@
 from jax.sharding import PartitionSpec as P
 
 HD = 64
+
+
+def drive_fields_on_mesh(u_in, array_dim, x_part):
+    r_now = u_in.shape
+    finding = u_in.reshape(
+        *r_now[:array_dim], x_part, r_now[array_dim] // x_part, *r_now[array_dim + 1 :]
+    )
+    return jnp.moveaxis(finding, array_dim, 0)
+
+
+def _list_cells(arr, on_dim):
+    arr = jnp.moveaxis(arr, 0, on_dim)
+    state_next = arr.shape
+    return arr.reshape(
+        *state_next[:on_dim], state_next[on_dim] * state_next[on_dim + 1], *state_next[on_dim + 2 :]
+    )
+
+
+def advance_side_on_mesh(my_tile, along_axis, view, own_rows):
+    kept_arr, tall = (lax.axis_size(along_axis), lax.axis_index(along_axis))
+    local_part = drive_fields_on_mesh(my_tile, view, kept_arr)
+    everything = local_part
+    for ix in range(1, kept_arr):
+        h_now, view_out = ((tall + ix) % kept_arr, (tall - ix) % kept_arr)
+        r1 = lax.dynamic_index_in_dim(local_part, h_now, 0)
+        outcome_arr = lax.ppermute(
+            r1,
+            axis_name=along_axis,
+            perm=list(map(lambda b: (b, (b + ix) % kept_arr), range(kept_arr))),
+        )
+        everything = lax.dynamic_update_slice_in_dim(everything, outcome_arr, view_out, axis=0)
+    return _list_cells(everything, own_rows)
 
 
 def per_device(tokens, norm_gain, w_query, w_keyval, w_out, kv_cache, lengths, dest_slot):
@@ -93,7 +125,7 @@
     )
     raw_blocks = kv_cache.reshape(layers, per_dev, block_len, lane_width)
     outgoing = jnp.take(raw_blocks, send_idx, axis=1)
-    incoming = lax.all_to_all(outgoing, ("group", "dp"), split_axis=1, concat_axis=1, tiled=True)
+    incoming = advance_side_on_mesh(outgoing, ("group", "dp"), 1, 1)
     where_from = senders * capacity + live_rank
     valid = (recv_all == my_index) & live_all
     slot_local = jnp.where(valid, dest_all - my_index * per_dev, per_dev)

time: 346 us -> 345 us (level)
  waiting for transfers between devices: 85.9 us -> 59.8 us
  local copies, waits for them, and re-layouts: 68.4 us -> 82.6 us
  starting transfers between devices: 4.64 us -> 14 us
    all_to_all x1 -> x0, waiting for transfers between devices: 46.2 us -> none  [per_device(): lax.all_to_all(outgoing, ('group', 'dp'), split_axis=1, concat_axis=1, ti...]
    ppermute x0 -> x7, waiting for transfers between devices: none -> 18.7 us  [advance_side_on_mesh(): lax.ppermute(r1, axis_name=along_axis, perm=list(map(lambda b: (b, (b + i...]
    ppermute x0 -> x7, starting transfers between devices: none -> 13.9 us  [advance_side_on_mesh(): lax.ppermute(r1, axis_name=along_axis, perm=list(map(lambda b: (b, (b + i...]
    dynamic_update_slice x0 -> x7, local copies, waits for them, and re-layouts: none -> 11.6 us  [advance_side_on_mesh(): lax.dynamic_update_slice_in_dim(everything, outcome_arr, view_out, axis=0)]
    gather x1 -> x2, local copies, waits for them, and re-layouts: 6.48 us -> 11.2 us  [per_device(): outgoing = jnp.take(raw_blocks, send_idx, axis=1)]
    all_to_all x1 -> x0, local copies, waits for them, and re-layouts: 4.73 us -> none  [per_device(): lax.all_to_all(outgoing, ('group', 'dp'), split_axis=1, concat_axis=1, ti...]
    transpose x0 -> x1, other arithmetic: none -> 4.64 us  [drive_fields_on_mesh(): return jnp.moveaxis(finding, array_dim, 0)]
    all_to_all x1 -> x0, starting transfers between devices: 4.6 us -> none  [per_device(): lax.all_to_all(outgoing, ('group', 'dp'), split_axis=1, concat_axis=1, ti...]
  transfers between devices with their start and end apart: 2 -> 8, of which waited for: 2 -> 4; matrix products, arithmetic and copies ran while one was open for 13% -> 18% of each run, Pallas kernels for 0% -> 0%
where the time goes in v1:
time: 345 us; the launch traced here: 344 us
  matrix products  86.4 us (25%)
  local copies, waits for them, and re-layouts  82.6 us (24%)
  other arithmetic  72.9 us (21%)
  waiting for transfers between devices  59.8 us (17%)
  between operations  14.4 us (4%)
  starting transfers between devices  14 us (4%)
  blocking collectives  10.3 us (3%)
    reduce_scatter x1, waiting for transfers between devices, per_device(): lax.psum_scatter(jnp.dot(attn, w_out, preferred_element_type=jnp.float32)...  41.1 us
    reduce_sum x4, other arithmetic, attend(): jnp.sum(expo, axis=-1, keepdims=True)  40.7 us
    dot_general x4, matrix products, attend(): jnp.einsum('kgct,tkd->ckgd', weights, pairs[:, :, 1], preferred_element_t...  36.2 us
    dot_general x4, matrix products, attend(): jnp.einsum('ckgd,tkd->kgct', query_p, pairs[:, :, 0], preferred_element_t...  35.9 us
    ppermute x7, waiting for transfers between devices, advance_side_on_mesh(): lax.ppermute(r1, axis_name=along_axis, perm=list(map(lambda b: (b, (b + i...  18.7 us
    unnamed x15, local copies, waits for them, and re-layouts  14.9 us
    ppermute x7, starting transfers between devices, advance_side_on_mesh(): lax.ppermute(r1, axis_name=along_axis, perm=list(map(lambda b: (b, (b + i...  13.9 us
    dynamic_update_slice x7, local copies, waits for them, and re-layouts, advance_side_on_mesh(): lax.dynamic_update_slice_in_dim(everything, outcome_arr, view_out, axis=0)  11.6 us
  transfers between devices with their start and end apart: 8, of which 4 were waited for; matrix products, arithmetic and copies ran while one was open for 18% of the time, Pallas kernels for 0%

profile of v1, /device:TPU:0, one launch (start us, length us, event | category | flops | bytes accessed | tf_op | source)
XLA Modules:
  0.0 343.6 jit_solution(7585218697769797410)
XLA Ops:
  7.2 1.4 slice_bitcast_fusion
  8.6 3.2 slice.25
  11.8 4.5 %copy.40 = bf16[1,4,16,128,128]{3,2,4,1,0:T(8,128)(2,1)} copy(bf16[1,4,16,128,128]{4,3,2,1,0:T(8,128)(2,1)} %slice.25) | data formatting | bytes 4194304 | tf_op jit(solution)/shard_map/slice | solution.py:63
  16.3 4.2 %reshape_squeeze.3 = bf16[4,2048,1,2,64]{1,4,3,2,0:T(8,128)(2,1)} reshape(bf16[1,4,16,128,128]{3,2,4,1,0:T(8,128)(2,1)} %copy.40) | data formatting | bytes 4194304 | tf_op jit(solution)/shard_map/reshape;squeeze | solution.py:63
  20.4 3.2 fusion.27
  23.9 2.3 fusion.33
  26.8 5.2 %convolution_convert_fusion = bf16[1024,512]{1,0:T(8,128)(2,1)S(1)} fusion(bf16[2048,512]{1,0:T(8,128)(2,1)} %param.12, bf16[1024,2048]{1,0:T(8,128)(2,1)} %param.10, f32[2048]{0:T(1024)S(1)} %convert_element_type.40, f32[1024]{0:T(1024)S(1)} %add_rsqrt_fusion), kind=kOutput, calls=%fused_computation.49 | convolution fusion | flops 2156396544 | bytes 7352320 | tf_op jit(solution)/shard_map/dot_general | solution.py:59
  32.1 2.1 reshape.496
  34.2 3.0 copy.44
  37.2 142.6 %while.14 = (s32[]{:T(128)}, bf16[4,256,512]{2,1,0:T(8,128)(2,1)}, s32[4]{0:T(128)}, bf16[4,2048,1,2,64]{1,4,3,2,0:T(8,128)(2,1)}, bf16[4,256,1,2,64]{1,4,3,2,0:...) while((s32[]{:T(128)}, bf16[4,256,512]{2,1,0:T(8,128)(2,1)}, ...), condition=%wide.region_4.5_spmd.clone.clone, body=%wide.region_1.4_spmd.clone.clone.sunk | while | flops 1268387072 | bytes 63510268 | solution.py:94
  37.2 1.3 dynamic_slice.126
  39.2 2.0 fusion.61
  41.3 1.1 dynamic-slice_bitcast_fusion.12
  42.4 9.0 %fusion.62 = (f32[8,256]{1,0:T(8,128)S(1)}, f32[2304,256,8]{1,0,2:T(8,128)}) fusion(pred[256,2304]{0,1:T(8,128)(4,1)S(1)} %fusion.61, bf16[4,256,1,8,64]{1,4,3,2,0:T(8,128)(2,1)} %get-tuple-element.308, s32[]{:T(128)S(6)} %copy.63, bf16[256,1,2,64]{0,3,2,1:T(8,128)(2,1)S(1)} %dynamic-slice_bitcast_fusion.11, ...), kind=kOutput, calls=%fused_computation.10.clone.1 | convolution fusion | flops 618723328 | bytes 20324356 | tf_op jit(solution)/shard_map/while/body/eval_jaxpr/ckgd,tkd->kgct/dot_general | solution.py:72
  51.4 10.2 %fusion.63 = f32[8,256]{1,0:T(8,128)S(1)} fusion(f32[2304,256,8]{1,0,2:T(8,128)} %get-tuple-element.282, f32[8,256]{1,0:T(8,128)S(1)} %get-tuple-element.283, pred[256,2304]{0,1:T(8,128)(4,1)S(1)} %fusion.61), kind=kLoop, calls=%fused_computation.9.clone.1 | loop fusion | flops 18872320 | bytes 19480576 | tf_op jit(solution)/shard_map/while/body/eval_jaxpr/reduce_sum | solution.py:85
  61.6 9.0 %fusion.64 = bf16[64,8,256]{2,0,1:T(8,128)(2,1)S(1)} fusion(f32[8,256]{1,0:T(8,128)S(1)} %fusion.63, f32[8,256]{1,0:T(8,128)S(1)} %get-tuple-element.283, f32[2304,256,8]{1,0,2:T(8,128)} %get-tuple-element.282, pred[256,2304]{0,1:T(8,128)(4,1)S(1)} %fusion.61, bf16[2048,1,2,64]{0,3,2,1:T(8,128)(2,1)S(1)} %dynamic-slice_bitcast_fusion.12, ...), kind=kOutput, calls=%fused_computation.17.clone.1 | convolution fusion | flops 628293632 | bytes 20332544 | tf_op jit(solution)/shard_map/while/body/eval_jaxpr/kgct,tkd->ckgd/dot_general | solution.py:86
  72.2 0.7 constant_dynamic-update-slice_fusion.9
  72.9 1.3 dynamic_slice.126
  74.9 2.0 fusion.61
  77.0 1.1 dynamic-slice_bitcast_fusion.12
  78.0 9.0 %fusion.62 = (f32[8,256]{1,0:T(8,128)S(1)}, f32[2304,256,8]{1,0,2:T(8,128)}) fusion(pred[256,2304]{0,1:T(8,128)(4,1)S(1)} %fusion.61, bf16[4,256,1,8,64]{1,4,3,2,0:T(8,128)(2,1)} %get-tuple-element.308, s32[]{:T(128)S(6)} %copy.63, bf16[256,1,2,64]{0,3,2,1:T(8,128)(2,1)S(1)} %dynamic-slice_bitcast_fusion.11, ...), kind=kOutput, calls=%fused_computation.10.clone.1 | convolution fusion | flops 618723328 | bytes 20324356 | tf_op jit(solution)/shard_map/while/body/eval_jaxpr/ckgd,tkd->kgct/dot_general | solution.py:72
  87.0 10.2 %fusion.63 = f32[8,256]{1,0:T(8,128)S(1)} fusion(f32[2304,256,8]{1,0,2:T(8,128)} %get-tuple-element.282, f32[8,256]{1,0:T(8,128)S(1)} %get-tuple-element.283, pred[256,2304]{0,1:T(8,128)(4,1)S(1)} %fusion.61), kind=kLoop, calls=%fused_computation.9.clone.1 | loop fusion | flops 18872320 | bytes 19480576 | tf_op jit(solution)/shard_map/while/body/eval_jaxpr/reduce_sum | solution.py:85
  97.2 9.0 %fusion.64 = bf16[64,8,256]{2,0,1:T(8,128)(2,1)S(1)} fusion(f32[8,256]{1,0:T(8,128)S(1)} %fusion.63, f32[8,256]{1,0:T(8,128)S(1)} %get-tuple-element.283, f32[2304,256,8]{1,0,2:T(8,128)} %get-tuple-element.282, pred[256,2304]{0,1:T(8,128)(4,1)S(1)} %fusion.61, bf16[2048,1,2,64]{0,3,2,1:T(8,128)(2,1)S(1)} %dynamic-slice_bitcast_fusion.12, ...), kind=kOutput, calls=%fused_computation.17.clone.1 | convolution fusion | flops 628293632 | bytes 20332544 | tf_op jit(solution)/shard_map/while/body/eval_jaxpr/kgct,tkd->ckgd/dot_general | solution.py:86
  107.8 0.7 constant_dynamic-update-slice_fusion.9
  108.6 1.3 dynamic_slice.126
  110.5 2.0 fusion.61
  112.6 1.1 dynamic-slice_bitcast_fusion.12
  113.7 9.0 %fusion.62 = (f32[8,256]{1,0:T(8,128)S(1)}, f32[2304,256,8]{1,0,2:T(8,128)}) fusion(pred[256,2304]{0,1:T(8,128)(4,1)S(1)} %fusion.61, bf16[4,256,1,8,64]{1,4,3,2,0:T(8,128)(2,1)} %get-tuple-element.308, s32[]{:T(128)S(6)} %copy.63, bf16[256,1,2,64]{0,3,2,1:T(8,128)(2,1)S(1)} %dynamic-slice_bitcast_fusion.11, ...), kind=kOutput, calls=%fused_computation.10.clone.1 | convolution fusion | flops 618723328 | bytes 20324356 | tf_op jit(solution)/shard_map/while/body/eval_jaxpr/ckgd,tkd->kgct/dot_general | solution.py:72
  122.7 10.2 %fusion.63 = f32[8,256]{1,0:T(8,128)S(1)} fusion(f32[2304,256,8]{1,0,2:T(8,128)} %get-tuple-element.282, f32[8,256]{1,0:T(8,128)S(1)} %get-tuple-element.283, pred[256,2304]{0,1:T(8,128)(4,1)S(1)} %fusion.61), kind=kLoop, calls=%fused_computation.9.clone.1 | loop fusion | flops 18872320 | bytes 19480576 | tf_op jit(solution)/shard_map/while/body/eval_jaxpr/reduce_sum | solution.py:85
  132.9 9.0 %fusion.64 = bf16[64,8,256]{2,0,1:T(8,128)(2,1)S(1)} fusion(f32[8,256]{1,0:T(8,128)S(1)} %fusion.63, f32[8,256]{1,0:T(8,128)S(1)} %get-tuple-element.283, f32[2304,256,8]{1,0,2:T(8,128)} %get-tuple-element.282, pred[256,2304]{0,1:T(8,128)(4,1)S(1)} %fusion.61, bf16[2048,1,2,64]{0,3,2,1:T(8,128)(2,1)S(1)} %dynamic-slice_bitcast_fusion.12, ...), kind=kOutput, calls=%fused_computation.17.clone.1 | convolution fusion | flops 628293632 | bytes 20332544 | tf_op jit(solution)/shard_map/while/body/eval_jaxpr/kgct,tkd->ckgd/dot_general | solution.py:86
  144.2 1.3 dynamic_slice.126
  146.2 2.0 fusion.61
  148.3 1.1 dynamic-slice_bitcast_fusion.12
  149.3 9.0 %fusion.62 = (f32[8,256]{1,0:T(8,128)S(1)}, f32[2304,256,8]{1,0,2:T(8,128)}) fusion(pred[256,2304]{0,1:T(8,128)(4,1)S(1)} %fusion.61, bf16[4,256,1,8,64]{1,4,3,2,0:T(8,128)(2,1)} %get-tuple-element.308, s32[]{:T(128)S(6)} %copy.63, bf16[256,1,2,64]{0,3,2,1:T(8,128)(2,1)S(1)} %dynamic-slice_bitcast_fusion.11, ...), kind=kOutput, calls=%fused_computation.10.clone.1 | convolution fusion | flops 618723328 | bytes 20324356 | tf_op jit(solution)/shard_map/while/body/eval_jaxpr/ckgd,tkd->kgct/dot_general | solution.py:72
  158.3 10.2 %fusion.63 = f32[8,256]{1,0:T(8,128)S(1)} fusion(f32[2304,256,8]{1,0,2:T(8,128)} %get-tuple-element.282, f32[8,256]{1,0:T(8,128)S(1)} %get-tuple-element.283, pred[256,2304]{0,1:T(8,128)(4,1)S(1)} %fusion.61), kind=kLoop, calls=%fused_computation.9.clone.1 | loop fusion | flops 18872320 | bytes 19480576 | tf_op jit(solution)/shard_map/while/body/eval_jaxpr/reduce_sum | solution.py:85
  168.5 9.0 %fusion.64 = bf16[64,8,256]{2,0,1:T(8,128)(2,1)S(1)} fusion(f32[8,256]{1,0:T(8,128)S(1)} %fusion.63, f32[8,256]{1,0:T(8,128)S(1)} %get-tuple-element.283, f32[2304,256,8]{1,0,2:T(8,128)} %get-tuple-element.282, pred[256,2304]{0,1:T(8,128)(4,1)S(1)} %fusion.61, bf16[2048,1,2,64]{0,3,2,1:T(8,128)(2,1)S(1)} %dynamic-slice_bitcast_fusion.12, ...), kind=kOutput, calls=%fused_computation.17.clone.1 | convolution fusion | flops 628293632 | bytes 20332544 | tf_op jit(solution)/shard_map/while/body/eval_jaxpr/kgct,tkd->ckgd/dot_general | solution.py:86
  179.9 6.8 %fusion.47 = f32[1024,2048]{1,0:T(8,128)} fusion(bf16[1024,512]{1,0:T(8,128)(2,1)} %bitcast.129, bf16[512,2048]{1,0:T(8,128)(2,1)S(1)} %copy-done), kind=kOutput, calls=%fused_computation.108 | convolution fusion | flops 2147483648 | bytes 11534336 | tf_op jit(solution)/shard_map/dot_general | solution.py:97
  187.5 10.3 %all-gather = s32[8,4,2]{1,2,0:T(2,128)S(1)} all-gather(s32[1,4,2]{1,2,0:T(2,128)S(1)} %bitcast.127), channel_id=1, replica_groups=mesh['group'=4,'dp'=2,'tensor'=4] {'group','dp'}, dimensions={0}, use_global_device_ids=true | all-gather | bytes 288 | tf_op jit(solution)/shard_map/all_gather | solution.py:113
  198.7 1.0 scatter_custom_fusion.1
  199.7 6.5 %gather_fusion = bf16[32,4,128,128]{3,2,1,0:T(8,128)(2,1)} fusion(bf16[4,64,128,128]{3,2,1,0:T(8,128)(2,1)} %bitcast.126, s32[1024]{0:T(1024)S(1)} %pad_clamp_fusion.1), kind=kCustom, calls=%fused_computation | custom fusion | bytes 8388736 | tf_op jit(solution)/shard_map/jit(_take)/gather | solution.py:127
  206.2 4.7 %copy.49 = bf16[4,32,128,128]{3,2,1,0:T(8,128)(2,1)} copy(bf16[4,32,128,128]{3,2,0,1:T(8,128)(2,1)} %bitcast.125) | data formatting | bytes 8388608 | tf_op jit(solution)/shard_map/jit(_take)/gather | solution.py:127
  211.0 2.7 broadcast_select_fusion
  213.7 1.6 dynamic-slice_bitcast_fusion.2
  215.6 1.5 collective-permute-start.1
  217.1 1.1 collective-permute-start.2
  218.2 1.5 collective-permute-start.3
  220.1 2.4 scatter_custom_fusion
  222.6 4.6 %fusion.52 = bf16[8,4,4,128,128]{4,3,2,0,1:T(8,128)(2,1)} fusion(bf16[4,8,4,128,128]{4,3,2,1,0:T(8,128)(2,1)} %bitcast.124, pred[8,4]{1,0:T(8,128)(4,1)S(1)} %broadcast_in_dim.91), kind=kLoop, calls=%fused_computation.109 | loop fusion | flops 2097152 | bytes 8388640 | tf_op jit(solution)/shard_map/transpose | solution.py:14
  227.4 2.5 collective-permute-done
  230.5 2.0 constant_dynamic-update-slice_fusion.7
  232.4 9.0 %collective-permute-start.6 = (bf16[1,4,4,128,128]{4,3,2,0,1:T(8,128)(2,1)S(1)}, bf16[1,4,4,128,128]{4,3,2,0,1:T(8,128)(2,1)S(1)}, u32[]{:S(2)}, u32[]{:S(2)}) collective-permute-start(bf16[1,4,4,128,128]{4,3,2,0,1:T(8,128)(2,1)S(1)} %get-tuple-element.224), channel_id=1, source_target_pairs={{0,28},{4,0},{8,4},{12,8},{16,12},{20,16},{24,20},{28,24},{1,29},{... | collective-permute-start | bytes 1572872 | tf_op jit(solution)/shard_map/ppermute | solution.py:32
  241.4 2.0 constant_dynamic-update-slice_fusion.6
  243.4 9.7 %collective-permute-done.2 = bf16[1,4,4,128,128]{4,3,2,0,1:T(8,128)(2,1)} collective-permute-done((bf16[1,4,4,128,128]{4,3,2,0,1:T(8,128)(2,1)}, bf16[1,4,4,128,128]{4,3,2,0,1:T(8,128)(2,1)}, u32[]{:S(2)}, u32[]{:S(2)}) %collective-permute-start.2) | collective-permute-done | bytes 524320 | tf_op jit(solution)/shard_map/ppermute | solution.py:32
  253.1 1.9 constant_dynamic-update-slice_fusion.5
  255.0 2.0 constant_dynamic-update-slice_fusion.4
  257.0 6.4 %collective-permute-done.4 = bf16[1,4,4,128,128]{4,3,2,0,1:T(8,128)(2,1)} collective-permute-done((bf16[1,4,4,128,128]{4,3,2,0,1:T(8,128)(2,1)}, bf16[1,4,4,128,128]{4,3,2,0,1:T(8,128)(2,1)}, u32[]{:S(2)}, u32[]{:S(2)}) %collective-permute-start.4) | collective-permute-done | bytes 524320 | tf_op jit(solution)/shard_map/ppermute | solution.py:32
  263.4 2.0 constant_dynamic-update-slice_fusion.3
  265.4 0.9 constant_dynamic-update-slice_fusion.2
  266.3 0.9 constant_dynamic-update-slice_fusion.1
  267.2 7.8 %gather_fusion.1 = bf16[64,4,128,128]{3,2,1,0:T(8,128)(2,1)} fusion(bf16[4,32,128,128]{3,2,1,0:T(8,128)(2,1)} %bitcast.122, s32[1024]{0:T(1024)S(1)} %pad_clamp_fusion), kind=kCustom, calls=%fused_computation.1 | custom fusion | bytes 16777472 | tf_op jit(solution)/shard_map/jit(_take)/gather | solution.py:137
  275.0 7.3 %select_bitcast_fusion = bf16[4,64,128,128]{3,2,0,1:T(8,128)(2,1)} fusion(bf16[64,4,128,128]{3,2,1,0:T(8,128)(2,1)} %gather_fusion.1, pred[64]{0:T(512)(128)(4,1)S(1)} %compare_and_fusion.1), kind=kLoop, calls=%fused_computation.47 | loop fusion | flops 4194304 | bytes 16777280 | tf_op jit(solution)/shard_map/jit(_take)/select_n | solution.py:137
  282.3 10.6 %copy.50 = bf16[4,64,128,128]{3,2,1,0:T(8,128)(2,1)} copy(bf16[4,64,128,128]{3,2,0,1:T(8,128)(2,1)} %select_bitcast_fusion) | data formatting | bytes 16777216
  292.9 41.1 %reduce-scatter.2.cloned.1.call-done = f32[256,2048]{1,0:T(8,128)} async-done(((f32[1024,2048]{1,0:T(8,128)}), f32[256,2048]{1,0:T(8,128)}) %reduce-scatter.2.cloned.1.call-update) | async-done | bytes 2097168 | tf_op jit(solution)/shard_map/reduce_scatter | solution.py:96
  334.0 2.7 convert_element_type.44
  (98 shorter events, 11.6 us)
Async XLA Ops:
  7.2 172.7 %copy-start = (bf16[512,2048]{1,0:T(8,128)(2,1)S(1)}, bf16[512,2048]{1,0:T(8,128)(2,1)}, u32[]{:S(2)}) copy-start(bf16[512,2048]{1,0:T(8,128)(2,1)} %param.14) | copy-start | bytes 6291460
  7.2 326.8 %reduce-scatter.2.cloned.1.call-start = ((), (), s32[]{:S(2)}) async-start(), calls=%async_computation.1 | async-start | bytes 10485760 | tf_op jit(solution)/shard_map/reduce_scatter | solution.py:96
  11.7 8.7 %copy-start.3 = (bf16[2048]{0:T(1024)(128)(2,1)S(1)}, bf16[2048]{0:T(1024)(128)(2,1)}, u32[]{:S(2)}) copy-start(bf16[2048]{0:T(1024)(128)(2,1)} %param.11) | copy-start | bytes 12292
  20.4 3.4 %copy-start.1 = (bf16[1024,2048]{1,0:T(8,128)(2,1)S(1)}, bf16[1024,2048]{1,0:T(8,128)(2,1)}, u32[]{:S(2)}) copy-start(bf16[1024,2048]{1,0:T(8,128)(2,1)} %param.10) | copy-start | bytes 12582916
  61.5 9.1 %copy-start.5 = (s32[4]{0:T(128)S(1)}, s32[4]{0:T(128)}, u32[]{:S(2)}) copy-start(s32[4]{0:T(128)} %get-tuple-element.304) | copy-start | bytes 52 | tf_op jit(solution)/shard_map/while
  97.2 9.1 %copy-start.5 = (s32[4]{0:T(128)S(1)}, s32[4]{0:T(128)}, u32[]{:S(2)}) copy-start(s32[4]{0:T(128)} %get-tuple-element.304) | copy-start | bytes 52 | tf_op jit(solution)/shard_map/while
  132.8 9.1 %copy-start.5 = (s32[4]{0:T(128)S(1)}, s32[4]{0:T(128)}, u32[]{:S(2)}) copy-start(s32[4]{0:T(128)} %get-tuple-element.304) | copy-start | bytes 52 | tf_op jit(solution)/shard_map/while
  168.5 9.1 %copy-start.5 = (s32[4]{0:T(128)S(1)}, s32[4]{0:T(128)}, u32[]{:S(2)}) copy-start(s32[4]{0:T(128)} %get-tuple-element.304) | copy-start | bytes 52 | tf_op jit(solution)/shard_map/while
  186.7 0.7 copy-start.2
  186.7 0.8 copy-start.4
  215.3 14.7 %collective-permute-start = (bf16[1,4,4,128,128]{4,3,2,0,1:T(8,128)(2,1)}, bf16[1,4,4,128,128]{4,3,2,0,1:T(8,128)(2,1)}, u32[]{:S(2)}, u32[]{:S(2)}) collective-permute-start(bf16[1,4,4,128,128]{4,3,2,0,1:T(8,128)(2,1)} %get-tuple-element.230), channel_id=1, source_target_pairs={{0,4},{4,8},{8,12},{12,16},{16,20},{20,24},{24,28},{28,0},{1,5},{5... | collective-permute-start | bytes 1572872 | tf_op jit(solution)/shard_map/ppermute | solution.py:32
  215.6 16.9 %collective-permute-start.1 = (bf16[1,4,4,128,128]{4,3,2,0,1:T(8,128)(2,1)}, bf16[1,4,4,128,128]{4,3,2,0,1:T(8,128)(2,1)}, u32[]{:S(2)}, u32[]{:S(2)}) collective-permute-start(bf16[1,4,4,128,128]{4,3,2,0,1:T(8,128)(2,1)} %get-tuple-element.229), channel_id=1, source_target_pairs={{0,8},{4,12},{8,16},{12,20},{16,24},{20,28},{24,0},{28,4},{1,9},{5... | collective-permute-start | bytes 1572872 | tf_op jit(solution)/shard_map/ppermute | solution.py:32
  217.1 36.0 %collective-permute-start.2 = (bf16[1,4,4,128,128]{4,3,2,0,1:T(8,128)(2,1)}, bf16[1,4,4,128,128]{4,3,2,0,1:T(8,128)(2,1)}, u32[]{:S(2)}, u32[]{:S(2)}) collective-permute-start(bf16[1,4,4,128,128]{4,3,2,0,1:T(8,128)(2,1)} %get-tuple-element.228), channel_id=1, source_target_pairs={{0,12},{4,16},{8,20},{12,24},{16,28},{20,0},{24,4},{28,8},{1,13},{... | collective-permute-start | bytes 1572872 | tf_op jit(solution)/shard_map/ppermute | solution.py:32
  218.2 36.8 %collective-permute-start.3 = (bf16[1,4,4,128,128]{4,3,2,0,1:T(8,128)(2,1)}, bf16[1,4,4,128,128]{4,3,2,0,1:T(8,128)(2,1)}, u32[]{:S(2)}, u32[]{:S(2)}) collective-permute-start(bf16[1,4,4,128,128]{4,3,2,0,1:T(8,128)(2,1)} %get-tuple-element.227), channel_id=1, source_target_pairs={{0,16},{4,20},{8,24},{12,28},{16,0},{20,4},{24,8},{28,12},{1,17},{... | collective-permute-start | bytes 1572872 | tf_op jit(solution)/shard_map/ppermute | solution.py:32
  219.7 43.7 %collective-permute-start.4 = (bf16[1,4,4,128,128]{4,3,2,0,1:T(8,128)(2,1)}, bf16[1,4,4,128,128]{4,3,2,0,1:T(8,128)(2,1)}, u32[]{:S(2)}, u32[]{:S(2)}) collective-permute-start(bf16[1,4,4,128,128]{4,3,2,0,1:T(8,128)(2,1)} %get-tuple-element.226), channel_id=1, source_target_pairs={{0,20},{4,24},{8,28},{12,0},{16,4},{20,8},{24,12},{28,16},{1,21},{... | collective-permute-start | bytes 1572872 | tf_op jit(solution)/shard_map/ppermute | solution.py:32
  229.9 35.5 %collective-permute-start.5 = (bf16[1,4,4,128,128]{4,3,2,0,1:T(8,128)(2,1)S(1)}, bf16[1,4,4,128,128]{4,3,2,0,1:T(8,128)(2,1)S(1)}, u32[]{:S(2)}, u32[]{:S(2)}) collective-permute-start(bf16[1,4,4,128,128]{4,3,2,0,1:T(8,128)(2,1)S(1)} %get-tuple-element.225), channel_id=1, source_target_pairs={{0,24},{4,28},{8,0},{12,4},{16,8},{20,12},{24,16},{28,20},{1,25},{... | collective-permute-start | bytes 1572872 | tf_op jit(solution)/shard_map/ppermute | solution.py:32
  232.4 33.8 %collective-permute-start.6 = (bf16[1,4,4,128,128]{4,3,2,0,1:T(8,128)(2,1)S(1)}, bf16[1,4,4,128,128]{4,3,2,0,1:T(8,128)(2,1)S(1)}, u32[]{:S(2)}, u32[]{:S(2)}) collective-permute-start(bf16[1,4,4,128,128]{4,3,2,0,1:T(8,128)(2,1)S(1)} %get-tuple-element.224), channel_id=1, source_target_pairs={{0,28},{4,0},{8,4},{12,8},{16,12},{20,16},{24,20},{28,24},{1,29},{... | collective-permute-start | bytes 1572872 | tf_op jit(solution)/shard_map/ppermute | solution.py:32
Sparse Core Ops, SparseCore 0:
  186.8 147.1 reduce-scatter.1
